TPU v7x, 256 devices: a whole 4x4x8 slice. The times are simulated.
256 devices in a mesh: dp: 32 (over z, y_hi, core), mp: 8 (over x, y_lo).
Axes of the slice: x: 4, y: 4 (y_hi: 2, y_lo: 2; y = y_hi * 2 + y_lo), z: 8, core: 2. Of those that a mesh axis runs over, the one named last changes fastest.
Arguments:
- token_ids: int32 [128, 64], P(None, 'dp'), may hold values from 0 to 1023
- fanout: int32 [128, 16], replicated, may hold values from 1 to 16
- table_of_column: int32 [64], P('dp'), may hold values from 0 to 15
- embed_table: bfloat16 [64, 1024, 1024], P('dp', 'mp'), may hold values from -35 to 35
- start_vector: bfloat16 [1024], replicated, may hold values from -6 to 6
- gain_attn: bfloat16 [1024], replicated, may hold values from 0.25 to 1.75
- gain_mlp: bfloat16 [1024], replicated, may hold values from 0.25 to 1.75
- gain_final: bfloat16 [1024], replicated, may hold values from 0.25 to 1.75
- w_qkv: bfloat16 [1024, 3, 1024], P(None, None, 'mp'), may hold values from -8 to 8
- w_out: bfloat16 [1024, 1024], P(None, 'mp'), may hold values from -0.1875 to 0.1875
- w_gate: bfloat16 [1024, 4096], P(None, 'mp'), may hold values from -0.1875 to 0.1875
- w_up: bfloat16 [1024, 4096], P(None, 'mp'), may hold values from -0.1875 to 0.1875
- w_down: bfloat16 [1024, 4096], P(None, 'mp'), may hold values from -0.09375 to 0.09375
Outputs:
- nll: float32 [128, 64], P(None, 'dp')
- grad_table: float32 [64, 1024, 1024], P('dp', 'mp')
- grad_qkv: float32 [1024, 3, 1024], P('dp', None, 'mp')
- grad_out: float32 [1024, 1024], P('dp', 'mp')
- grad_gate: float32 [1024, 4096], P('dp', 'mp')
- grad_up: float32 [1024, 4096], P('dp', 'mp')
- grad_down: float32 [1024, 4096], P('dp', 'mp')
All inputs are finite; a program needn't handle non-finite values.
Results may differ from a plain program's by a relative error of at most 0.015.
The roundings to bfloat16 on the way count: a program that leaves them out, or rounds other values in their place, can miss the bound.
Values may be sent and summed in bfloat16 or wider, within the bound.
A program may use at most 128 MiB of HBM per device.

v0:
```python
import math
import jax
import jax.numpy as jnp
from jax import lax
from jax.sharding import PartitionSpec as P

HS = 64
TABLES = 16
EPS = 1e-05
ATTN_CAP = 50.0
LOGIT_CAP = 30.0


def gather_features(values):
    return lax.all_gather(values, "mp", axis=2, tiled=True)


def feature_sum(term):
    return lax.psum_scatter(term, "mp", scatter_dimension=2, tiled=True)


def cols_to_rows(values):
    return lax.all_to_all(values, "dp", split_axis=0, concat_axis=1, tiled=True)


def rows_to_cols(values):
    return lax.all_to_all(values, "dp", split_axis=1, concat_axis=0, tiled=True)


def rms_of(values):
    floats = values.astype(jnp.float32)
    return jnp.sqrt(jnp.mean(floats * floats, axis=-1, keepdims=True) + EPS)


def normalize(values, gain, rms):
    return (values.astype(jnp.float32) / rms * gain.astype(jnp.float32)).astype(jnp.bfloat16)


def norm_back_full(values, d_norm, gain, rms):
    floats = values.astype(jnp.float32)
    gains = gain.astype(jnp.float32)
    total = jnp.sum(gains * d_norm * floats, axis=-1, keepdims=True)
    return gains * d_norm / rms - floats * total / (floats.shape[-1] * rms * rms * rms)


def norm_back_part(values, d_norm, gain, rms, model_width):
    floats = values.astype(jnp.float32)
    gains = gain.astype(jnp.float32)
    partial_total = jnp.sum(gains * d_norm * floats, axis=-1)
    total = lax.psum(partial_total, "mp")[..., None]
    return gains * d_norm / rms - floats * total / (model_width * rms * rms * rms)


def local(
    token_ids,
    fanout,
    table_of_column,
    embed_table,
    start_vector,
    gain_attn,
    gain_mlp,
    gain_final,
    w_qkv,
    w_out,
    w_gate,
    w_up,
    w_down,
):
    fl = jnp.float32
    mp_rank = lax.axis_index("mp")
    mp_count = lax.axis_size("mp")
    model_width = embed_table.shape[2]
    vocab_part = embed_table.shape[1]
    part_width = model_width // mp_count
    head_cols = w_qkv.shape[2]
    local_heads = head_cols // HS
    row_total_count = token_ids.shape[0]

    def own_part(vector):
        return lax.dynamic_slice_in_dim(vector, mp_rank * part_width, part_width, 0)

    local_ids = token_ids - mp_rank * vocab_part
    onehot = (
        local_ids[:, :, None] == jnp.arange(vocab_part, dtype=jnp.int32)[None, None, :]
    ).astype(jnp.bfloat16)
    picked = jnp.einsum("rcv,cvd->rcd", onehot, embed_table, preferred_element_type=fl)
    emb_cols = feature_sum(picked).astype(jnp.bfloat16)
    emb_rows = cols_to_rows(emb_cols)
    rows_here = emb_rows.shape[0]
    col_count = emb_rows.shape[1]
    start_rows = jnp.broadcast_to(own_part(start_vector)[None, None, :], (rows_here, 1, part_width))
    resid_in = jnp.concatenate([start_rows, emb_rows[:, :-1]], axis=1)
    in_full = gather_features(resid_in)
    rms_attn = rms_of(in_full)
    norm_attn = normalize(in_full, gain_attn, rms_attn)
    qkv = jnp.einsum("rpd,dtx->rptx", norm_attn, w_qkv, preferred_element_type=fl).astype(
        jnp.bfloat16
    )
    queries = qkv[:, :, 0].reshape(rows_here, col_count, local_heads, HS)
    key_rows = qkv[:, :, 1].reshape(rows_here, col_count, local_heads, HS)
    value_rows = qkv[:, :, 2].reshape(rows_here, col_count, local_heads, HS)
    score_raw = jnp.einsum(
        "rqhe,rkhe->rhqk", queries, key_rows, preferred_element_type=fl
    ) / math.sqrt(HS)
    score = ATTN_CAP * jnp.tanh(score_raw / ATTN_CAP)
    col_index = jnp.arange(col_count, dtype=jnp.int32)
    causal = col_index[:, None] >= col_index[None, :]
    exp_score = jnp.where(causal, jnp.exp(score), 0.0)
    attn_prob = exp_score / jnp.sum(exp_score, axis=-1, keepdims=True)
    prob_b = attn_prob.astype(jnp.bfloat16)
    attn_heads = jnp.einsum(
        "rhqk,rkhe->rqhe", prob_b, value_rows, preferred_element_type=fl
    ).astype(jnp.bfloat16)
    attn_out = attn_heads.reshape(rows_here, col_count, head_cols)
    mixed_part = jnp.einsum("rpj,dj->rpd", attn_out, w_out, preferred_element_type=fl)
    resid_mid = (resid_in.astype(fl) + feature_sum(mixed_part)).astype(jnp.bfloat16)
    mid_full = gather_features(resid_mid)
    rms_mlp = rms_of(mid_full)
    norm_mlp = normalize(mid_full, gain_mlp, rms_mlp)
    gate_pre = jnp.einsum("rpd,df->rpf", norm_mlp, w_gate, preferred_element_type=fl)
    up_proj = jnp.einsum("rpd,df->rpf", norm_mlp, w_up, preferred_element_type=fl)
    hidden = (jax.nn.silu(gate_pre) * up_proj).astype(jnp.bfloat16)
    down_part = jnp.einsum("rpf,df->rpd", hidden, w_down, preferred_element_type=fl)
    resid_out = (resid_mid.astype(fl) + feature_sum(down_part)).astype(jnp.bfloat16)
    out_cols = rows_to_cols(resid_out)
    out_full = gather_features(out_cols)
    rms_final = rms_of(out_full)
    norm_final = normalize(out_full, gain_final, rms_final)
    width_root = math.sqrt(model_width)
    logit_raw = (
        jnp.einsum("rcd,cvd->rcv", norm_final, embed_table, preferred_element_type=fl) / width_root
    )
    capped = LOGIT_CAP * jnp.tanh(logit_raw / LOGIT_CAP)
    exp_logit = jnp.exp(capped)
    onehot_f = onehot.astype(fl)
    exp_total, target_logit = lax.psum(
        (jnp.sum(exp_logit, axis=-1), jnp.sum(capped * onehot_f, axis=-1)), "mp"
    )
    nll = jnp.log(exp_total) - target_logit
    select = table_of_column[None, :, None] == jnp.arange(TABLES, dtype=jnp.int32)[None, None, :]
    counts = jnp.sum(jnp.where(select, fanout[:, None, :], 0), axis=-1).astype(fl)
    row_scale = 1.0 / (counts * row_total_count)
    ratio = capped / LOGIT_CAP
    d_logit = (
        (exp_logit / exp_total[:, :, None] - onehot_f)
        * row_scale[:, :, None]
        * (1.0 - ratio * ratio)
    ).astype(jnp.bfloat16)
    d_final_part = (
        jnp.einsum("rcv,cvd->rcd", d_logit, embed_table, preferred_element_type=fl) / width_root
    )
    table_grad = (
        jnp.einsum("rcv,rcd->cvd", d_logit, norm_final, preferred_element_type=fl) / width_root
    )
    d_final = lax.psum(d_final_part, "mp")
    back_full = norm_back_full(out_full, d_final, gain_final, rms_final)
    d_out_cols = lax.dynamic_slice_in_dim(back_full, mp_rank * part_width, part_width, 2).astype(
        jnp.bfloat16
    )
    d_out = cols_to_rows(d_out_cols)
    d_out_full = gather_features(d_out)
    d_hidden = jnp.einsum("rpd,df->rpf", d_out_full, w_down, preferred_element_type=fl)
    sigmoid_gate = jax.nn.sigmoid(gate_pre)
    d_gate = (d_hidden * up_proj * sigmoid_gate * (1.0 + gate_pre * (1.0 - sigmoid_gate))).astype(
        jnp.bfloat16
    )
    d_up = (d_hidden * gate_pre * sigmoid_gate).astype(jnp.bfloat16)
    d_norm_mlp = jnp.einsum("rpf,df->rpd", d_gate, w_gate, preferred_element_type=fl) + jnp.einsum(
        "rpf,df->rpd", d_up, w_up, preferred_element_type=fl
    )
    d_mid = (
        d_out.astype(fl)
        + norm_back_part(
            resid_mid, feature_sum(d_norm_mlp), own_part(gain_mlp), rms_mlp, model_width
        )
    ).astype(jnp.bfloat16)
    mid_grad_full = gather_features(d_mid)
    d_attn = jnp.einsum("rpd,dj->rpj", mid_grad_full, w_out, preferred_element_type=fl).astype(
        jnp.bfloat16
    )
    d_attn = d_attn.reshape(rows_here, col_count, local_heads, HS)
    d_prob = jnp.einsum("rqhe,rkhe->rhqk", d_attn, value_rows, preferred_element_type=fl)
    ratio_s = score / ATTN_CAP
    d_score = attn_prob * (d_prob - jnp.sum(attn_prob * d_prob, axis=-1, keepdims=True))
    d_scaled = (d_score * (1.0 - ratio_s * ratio_s) / math.sqrt(HS)).astype(jnp.bfloat16)
    d_query = jnp.einsum("rhqk,rkhe->rqhe", d_scaled, key_rows, preferred_element_type=fl)
    d_key = jnp.einsum("rhqk,rqhe->rkhe", d_scaled, queries, preferred_element_type=fl)
    d_value = jnp.einsum("rhqk,rqhe->rkhe", prob_b, d_attn, preferred_element_type=fl)
    d_qkv = (
        jnp.stack([d_query, d_key, d_value], axis=2)
        .reshape(rows_here, col_count, 3, head_cols)
        .astype(jnp.bfloat16)
    )
    d_norm_attn = jnp.einsum("rptx,dtx->rpd", d_qkv, w_qkv, preferred_element_type=fl)
    d_in = (
        d_mid.astype(fl)
        + norm_back_part(
            resid_in, feature_sum(d_norm_attn), own_part(gain_attn), rms_attn, model_width
        )
    ).astype(jnp.bfloat16)
    d_embed_rows = jnp.concatenate(
        [d_in[:, 1:], jnp.zeros((rows_here, 1, part_width), jnp.bfloat16)], axis=1
    )
    d_embed_cols = rows_to_cols(d_embed_rows)
    d_embed_full = gather_features(d_embed_cols)
    table_grad = table_grad + jnp.einsum(
        "rcv,rcd->cvd", onehot, d_embed_full, preferred_element_type=fl
    )
    qkv_term = jnp.einsum("rpd,rptx->dtx", norm_attn, d_qkv, preferred_element_type=fl).reshape(
        model_width, 3 * head_cols
    )
    out_term = jnp.einsum("rpd,rpj->dj", mid_grad_full, attn_out, preferred_element_type=fl)
    whole_terms = jnp.concatenate(
        [
            jnp.concatenate([qkv_term, out_term], axis=1),
            jnp.concatenate(
                [
                    jnp.einsum("rpd,rpf->df", norm_mlp, d_gate, preferred_element_type=fl),
                    jnp.einsum("rpd,rpf->df", norm_mlp, d_up, preferred_element_type=fl),
                    jnp.einsum("rpd,rpf->df", d_out_full, hidden, preferred_element_type=fl),
                ],
                axis=1,
            ),
        ],
        axis=1,
    )
    summed = lax.psum_scatter(whole_terms, "dp", scatter_dimension=0, tiled=True)
    ff_part = w_gate.shape[1]
    qkv_width = 3 * head_cols
    grad_qkv = summed[:, :qkv_width].reshape(summed.shape[0], 3, head_cols)
    grad_out = summed[:, qkv_width : qkv_width + head_cols]
    base = qkv_width + head_cols
    grad_gate = summed[:, base : base + ff_part]
    grad_up = summed[:, base + ff_part : base + 2 * ff_part]
    grad_down = summed[:, base + 2 * ff_part : base + 3 * ff_part]
    return (nll, table_grad, grad_qkv, grad_out, grad_gate, grad_up, grad_down)


def solution(mesh):
    return jax.shard_map(
        local,
        mesh=mesh,
        in_specs=(
            P(None, "dp"),
            P(),
            P("dp"),
            P("dp", "mp", None),
            P(),
            P(),
            P(),
            P(),
            P(None, None, "mp"),
            P(None, "mp"),
            P(None, "mp"),
            P(None, "mp"),
            P(None, "mp"),
        ),
        out_specs=(
            P(None, "dp"),
            P("dp", "mp", None),
            P("dp", None, "mp"),
            P("dp", "mp"),
            P("dp", "mp"),
            P("dp", "mp"),
            P("dp", "mp"),
        ),
        check_vma=False,
    )
```

profile of v0, /device:TPU:2, one launch (start us, length us, event | category | flops | bytes accessed | tf_op | source)
XLA Modules:
  0.0 726.3 jit_solution(7134462608592402723)
XLA Ops:
  8.0 2.4 convolution_bitcast_fusion
  10.4 44.1 %reduce-scatter.9.cloned.1.call-done = f32[128,2,128]{2,0,1:T(8,128)} async-done(((f32[128,2,1024]{2,0,1:T(8,128)}), f32[128,2,128]{2,0,1:T(8,128)}) %reduce-scatter.9.cloned.1.call-update) | async-done | bytes 131088 | tf_op jit(solution)/shard_map/reduce_scatter | solution.py:19
  56.1 10.0 %all-to-all-start = ((bf16[128,2,128]{2,1,0:T(2,128)(2,1)}), bf16[128,2,128]{2,1,0:T(2,128)(2,1)S(1)}, u32[]{:S(2)}, u32[]{:S(2)}) async-start(bf16[128,2,128]{2,1,0:T(2,128)(2,1)} %copy.114), calls=%async_computation.1 | async-start | bytes 131072 | tf_op jit(solution)/shard_map/all_to_all | solution.py:23
  67.7 8.4 %all-to-all-done = bf16[128,2,128]{2,1,0:T(2,128)(2,1)S(1)} async-done(((bf16[128,2,128]{2,1,0:T(2,128)(2,1)}), bf16[128,2,128]{2,1,0:T(2,128)(2,1)S(1)}, u32[]{:S(2)}, u32[]{:S(2)}) %all-to-all-start) | async-done | bytes 65568 | tf_op jit(solution)/shard_map/all_to_all | solution.py:23
  76.8 26.7 %all_gather.18 = bf16[4,64,1024]{2,1,0:T(8,128)(2,1)S(1)} all-gather(bf16[4,64,128]{2,1,0:T(8,128)(2,1)S(1)} %get-tuple-element.52), channel_id=1, replica_groups=mesh['dp'=32,'mp'=8] {'mp'}, dimensions={2}, use_global_device_ids=true | all-gather | bytes 589824 | tf_op jit(solution)/shard_map/all_gather | solution.py:15
  108.4 34.5 %reduce-scatter.11.cloned.1.call-done = f32[4,64,128]{2,1,0:T(8,128)} async-done(((f32[4,64,1024]{2,1,0:T(8,128)}), f32[4,64,128]{2,1,0:T(8,128)}) %reduce-scatter.11.cloned.1.call-update) | async-done | bytes 131088 | tf_op jit(solution)/shard_map/reduce_scatter | solution.py:19
  143.8 26.9 %all_gather.19 = bf16[4,64,1024]{2,1,0:T(8,128)(2,1)S(1)} all-gather(bf16[4,64,128]{2,1,0:T(8,128)(2,1)S(1)} %add_convert_fusion), channel_id=1, replica_groups=mesh['dp'=32,'mp'=8] {'mp'}, dimensions={2}, use_global_device_ids=true | all-gather | bytes 589824 | tf_op jit(solution)/shard_map/all_gather | solution.py:15
  174.1 2.5 multiply_convert_fusion.3
  178.3 40.9 %reduce-scatter.13.cloned.1.call-done = f32[4,64,128]{2,1,0:T(8,128)} async-done(((f32[4,64,1024]{2,1,0:T(8,128)}), f32[4,64,128]{2,1,0:T(8,128)}) %reduce-scatter.13.cloned.1.call-update) | async-done | bytes 131088 | tf_op jit(solution)/shard_map/reduce_scatter | solution.py:19
  220.9 10.0 %all-to-all-start.1 = ((bf16[4,64,128]{2,0,1:T(4,128)(2,1)}), bf16[4,64,128]{2,0,1:T(4,128)(2,1)S(1)}, u32[]{:S(2)}, u32[]{:S(2)}) async-start(bf16[4,64,128]{2,0,1:T(4,128)(2,1)} %copy.121), calls=%async_computation.4 | async-start | bytes 131072 | tf_op jit(solution)/shard_map/all_to_all | solution.py:27
  231.5 9.3 %all-to-all-done.1 = bf16[4,64,128]{2,0,1:T(4,128)(2,1)S(1)} async-done(((bf16[4,64,128]{2,0,1:T(4,128)(2,1)}), bf16[4,64,128]{2,0,1:T(4,128)(2,1)S(1)}, u32[]{:S(2)}, u32[]{:S(2)}) %all-to-all-start.1) | async-done | bytes 65568 | tf_op jit(solution)/shard_map/all_to_all | solution.py:27
  240.9 26.7 %all_gather.20 = bf16[128,2,1024]{2,0,1:T(8,128)(2,1)S(1)} all-gather(bf16[128,2,128]{2,0,1:T(8,128)(2,1)S(1)} %bitcast.144), channel_id=1, replica_groups=mesh['dp'=32,'mp'=8] {'mp'}, dimensions={2}, use_global_device_ids=true | all-gather | bytes 589824 | tf_op jit(solution)/shard_map/all_gather | solution.py:15
  269.9 14.4 %psum.35 = f32[128,2]{0,1:T(2,128)S(1)} all-reduce(f32[128,2]{0,1:T(2,128)} %get-tuple-element.35), channel_id=1, replica_groups=mesh['dp'=32,'mp'=8] {'mp'}, use_global_device_ids=true, to_apply=%region_8.9 | all-reduce | flops 256 | bytes 2048 | tf_op jit(solution)/shard_map/psum | solution.py:136
  287.8 76.1 %all-reduce.4.cloned.1.call-done = f32[128,2,1024]{2,0,1:T(8,128)} async-done(((f32[128,2,1024]{2,0,1:T(8,128)}), f32[128,2,1024]{2,0,1:T(8,128)}) %all-reduce.4.cloned.1.call-update) | async-done | bytes 1048592 | tf_op jit(solution)/shard_map/psum | solution.py:155
  366.6 19.4 %all_to_all.72 = bf16[128,2,128]{2,1,0:T(2,128)(2,1)S(1)} all-to-all(bf16[128,2,128]{2,1,0:T(2,128)(2,1)S(1)} %copy.124), channel_id=1, replica_groups=mesh['dp'=32,'mp'=8] {'dp'}, dimensions={0} | all-to-all | bytes 131072 | tf_op jit(solution)/shard_map/all_to_all | solution.py:23
  386.1 26.0 %all_gather.21 = bf16[4,64,1024]{2,1,0:T(8,128)(2,1)S(1)} all-gather(bf16[4,64,128]{2,1,0:T(8,128)(2,1)S(1)} %bitcast.138), channel_id=1, replica_groups=mesh['dp'=32,'mp'=8] {'mp'}, dimensions={2}, use_global_device_ids=true | all-gather | bytes 589824 | tf_op jit(solution)/shard_map/all_gather | solution.py:15
  417.6 33.3 %reduce-scatter.15.cloned.1.call-done = f32[4,64,128]{2,1,0:T(8,128)} async-done(((f32[4,64,1024]{2,1,0:T(8,128)}), f32[4,64,128]{2,1,0:T(8,128)}) %reduce-scatter.15.cloned.1.call-update) | async-done | bytes 131088 | tf_op jit(solution)/shard_map/reduce_scatter | solution.py:19
  452.5 18.0 %psum.38 = f32[4,64]{1,0:T(4,128)} all-reduce(f32[4,64]{1,0:T(4,128)} %fusion.46), channel_id=1, replica_groups=mesh['dp'=32,'mp'=8] {'mp'}, use_global_device_ids=true, to_apply=%region_16.17 | all-reduce | flops 256 | bytes 2048 | tf_op jit(solution)/shard_map/psum | solution.py:50
  472.2 27.0 %all_gather.22 = bf16[4,64,1024]{2,1,0:T(8,128)(2,1)S(1)} all-gather(bf16[4,64,128]{2,1,0:T(8,128)(2,1)S(1)} %fusion.61), channel_id=1, replica_groups=mesh['dp'=32,'mp'=8] {'mp'}, dimensions={2}, use_global_device_ids=true | all-gather | bytes 589824 | tf_op jit(solution)/shard_map/all_gather | solution.py:15
  506.3 2.2 convolution_convert_fusion.2
  510.7 2.6 convolution_bitcast_fusion.1
  513.6 2.7 bitcast_dynamic-update-slice_fusion.3
  518.2 2.8 bitcast_dynamic-update-slice_fusion.2
  521.1 2.6 bitcast_dynamic-update-slice_fusion.1
  525.4 9.2 %copy.156 = f32[1024,2048]{1,0:T(8,128)} copy(f32[1024,2048]{0,1:T(8,128)} %bitcast_dynamic-update-slice_fusion) | data formatting | bytes 16777216
  537.2 17.6 %reduce-scatter.17.cloned.1.call-done = f32[4,64,128]{2,1,0:T(8,128)} async-done(((f32[4,64,1024]{2,1,0:T(8,128)}), f32[4,64,128]{2,1,0:T(8,128)}) %reduce-scatter.17.cloned.1.call-update) | async-done | bytes 131088 | tf_op jit(solution)/shard_map/reduce_scatter | solution.py:19
  555.9 17.3 %all-reduce.1 = (f32[128,2]{0,1:T(2,128)S(1)}, f32[4,64]{1,0:T(4,128)S(1)}) all-reduce(f32[128,2]{0,1:T(2,128)S(1)} %copy-done.36, f32[4,64]{1,0:T(4,128)S(1)} %get-tuple-element.39), channel_id=1, replica_groups=mesh['dp'=32,'mp'=8] {'mp'}, use_global_device_ids=true, to_apply=%region_10.11 | all-reduce | flops 512 | bytes 4096 | tf_op jit(solution)/shard_map/psum | solution.py:136
  574.1 10.0 %all-to-all-start.3 = ((bf16[4,64,128]{2,0,1:T(4,128)(2,1)}), bf16[4,64,128]{2,0,1:T(4,128)(2,1)S(1)}, u32[]{:S(2)}, u32[]{:S(2)}) async-start(bf16[4,64,128]{2,0,1:T(4,128)(2,1)} %concatenate.12.clone), calls=%async_computation.8 | async-start | bytes 131072 | tf_op jit(solution)/shard_map/all_to_all | solution.py:27
  584.6 9.4 %all-to-all-done.3 = bf16[4,64,128]{2,0,1:T(4,128)(2,1)S(1)} async-done(((bf16[4,64,128]{2,0,1:T(4,128)(2,1)}), bf16[4,64,128]{2,0,1:T(4,128)(2,1)S(1)}, u32[]{:S(2)}, u32[]{:S(2)}) %all-to-all-start.3) | async-done | bytes 65568 | tf_op jit(solution)/shard_map/all_to_all | solution.py:27
  594.0 28.0 %all_gather.23 = bf16[128,2,1024]{2,0,1:T(8,128)(2,1)S(1)} all-gather(bf16[128,2,128]{2,0,1:T(8,128)(2,1)S(1)} %bitcast.145), channel_id=1, replica_groups=mesh['dp'=32,'mp'=8] {'mp'}, dimensions={2}, use_global_device_ids=true | all-gather | bytes 589824 | tf_op jit(solution)/shard_map/all_gather | solution.py:15
  622.0 2.5 convolution_add_fusion
  624.5 90.4 %reduce-scatter.19.cloned.1.call-done = f32[32,2048]{1,0:T(8,128)} async-done(((f32[1024,2048]{1,0:T(8,128)}), f32[32,2048]{1,0:T(8,128)}) %reduce-scatter.19.cloned.1.call-update) | async-done | bytes 262160
  (169 shorter events, 57.8 us)
Async XLA Ops:
  7.2 169.5 %copy-start = (bf16[1024,512]{1,0:T(8,128)(2,1)S(1)}, bf16[1024,512]{1,0:T(8,128)(2,1)}, u32[]{:S(2)}) copy-start(bf16[1024,512]{1,0:T(8,128)(2,1)} %param.25) | copy-start | bytes 3145732
  7.2 99.8 %copy-start.6 = (bf16[1024,128]{1,0:T(8,128)(2,1)S(1)}, bf16[1024,128]{1,0:T(8,128)(2,1)}, u32[]{:S(2)}) copy-start(bf16[1024,128]{1,0:T(8,128)(2,1)} %param.22) | copy-start | bytes 786436
  7.2 101.1 %copy-start.35 = (bf16[1024]{0:T(1024)(128)(2,1)S(1)}, bf16[1024]{0:T(1024)(128)(2,1)}, u32[]{:S(2)}) copy-start(bf16[1024]{0:T(1024)(128)(2,1)} %param.19) | copy-start | bytes 6148
  7.2 47.3 %reduce-scatter.9.cloned.1.call-start = ((), (), s32[]{:S(2)}) async-start(), calls=%async_computation.10 | async-start | bytes 1179648 | tf_op jit(solution)/shard_map/reduce_scatter | solution.py:19
  56.1 20.0 %all-to-all-start = ((bf16[128,2,128]{2,1,0:T(2,128)(2,1)}), bf16[128,2,128]{2,1,0:T(2,128)(2,1)S(1)}, u32[]{:S(2)}, u32[]{:S(2)}) async-start(bf16[128,2,128]{2,1,0:T(2,128)(2,1)} %copy.114), calls=%async_computation.1 | async-start | bytes 131072 | tf_op jit(solution)/shard_map/all_to_all | solution.py:23
  66.1 76.7 %reduce-scatter.11.cloned.1.call-start = ((), (), s32[]{:S(2)}) async-start(), calls=%async_computation.11 | async-start | bytes 1179648 | tf_op jit(solution)/shard_map/reduce_scatter | solution.py:19
  66.9 39.3 %copy-start.30 = (f32[1024]{0:T(1024)}, f32[1024]{0:T(1024)S(1)}, u32[]{:S(2)}) copy-start(f32[1024]{0:T(1024)S(1)} %convert_element_type.117) | copy-start | bytes 12292
  67.7 76.2 %copy-start.28 = (pred[64,64]{0,1:T(8,128)(4,1)}, pred[64,64]{0,1:T(8,128)(4,1)S(1)}, u32[]{:S(2)}) copy-start(pred[64,64]{0,1:T(8,128)(4,1)S(1)} %iota_compare_fusion.3) | copy-start | bytes 12292
  106.1 36.8 %copy-start.21 = (bf16[4,64,1,128]{1,3,0,2:T(8,128)(2,1)}, bf16[4,64,1,128]{1,3,0,2:T(8,128)(2,1)S(1)}, u32[]{:S(2)}) copy-start(bf16[4,64,1,128]{1,3,0,2:T(8,128)(2,1)S(1)} %copy.165) | copy-start | bytes 196612
  106.2 36.7 %copy-start.13 = (bf16[4,64,2,64]{3,2,1,0:T(2,128)(2,1)}, bf16[4,64,2,64]{3,2,1,0:T(2,128)(2,1)S(1)}, u32[]{:S(2)}) copy-start(bf16[4,64,2,64]{3,2,1,0:T(2,128)(2,1)S(1)} %reshape_squeeze.9) | copy-start | bytes 196612
  106.4 36.5 %copy-start.22 = (bf16[4,64,1,128]{1,3,0,2:T(8,128)(2,1)}, bf16[4,64,1,128]{1,3,0,2:T(8,128)(2,1)S(1)}, u32[]{:S(2)}) copy-start(bf16[4,64,1,128]{1,3,0,2:T(8,128)(2,1)S(1)} %copy.164) | copy-start | bytes 196612
  106.7 64.0 %copy-start.39 = (f32[4,2,64]{2,1,0:T(2,128)}, f32[4,2,64]{2,1,0:T(2,128)S(1)}, u32[]{:S(2)}) copy-start(f32[4,2,64]{2,1,0:T(2,128)S(1)} %get-tuple-element.59) | copy-start | bytes 6148
  106.9 35.9 %copy-start.14 = (bf16[4,2,64,64]{3,2,1,0:T(8,128)(2,1)}, bf16[4,2,64,64]{3,2,1,0:T(8,128)(2,1)S(1)}, u32[]{:S(2)}) copy-start(bf16[4,2,64,64]{3,2,1,0:T(8,128)(2,1)S(1)} %convolution_convert_fusion.4) | copy-start | bytes 196612
  108.3 111.0 %reduce-scatter.13.cloned.1.call-start = ((), (), s32[]{:S(2)}) async-start(), calls=%async_computation.12 | async-start | bytes 1179648 | tf_op jit(solution)/shard_map/reduce_scatter | solution.py:19
  108.4 69.7 %copy-start.31 = (f32[1024]{0:T(1024)}, f32[1024]{0:T(1024)S(1)}, u32[]{:S(2)}) copy-start(f32[1024]{0:T(1024)S(1)} %convert_element_type.126) | copy-start | bytes 12292
  171.5 96.8 %copy-start.1 = (bf16[2,128,1024]{2,1,0:T(8,128)(2,1)S(1)}, bf16[2,128,1024]{2,1,0:T(8,128)(2,1)}, u32[]{:S(2)}) copy-start(bf16[2,128,1024]{2,1,0:T(8,128)(2,1)} %param.16) | copy-start | bytes 1572868
  176.7 64.2 %copy-start.7 = (bf16[4,64,512]{2,1,0:T(8,128)(2,1)}, bf16[4,64,512]{2,1,0:T(8,128)(2,1)S(1)}, u32[]{:S(2)}) copy-start(bf16[4,64,512]{2,1,0:T(8,128)(2,1)S(1)} %get-tuple-element.61) | copy-start | bytes 786436
  220.9 20.0 %all-to-all-start.1 = ((bf16[4,64,128]{2,0,1:T(4,128)(2,1)}), bf16[4,64,128]{2,0,1:T(4,128)(2,1)S(1)}, u32[]{:S(2)}, u32[]{:S(2)}) async-start(bf16[4,64,128]{2,0,1:T(4,128)(2,1)} %copy.121), calls=%async_computation.4 | async-start | bytes 131072 | tf_op jit(solution)/shard_map/all_to_all | solution.py:27
  230.9 133.0 %all-reduce.4.cloned.1.call-start = ((), (), s32[]{:S(2)}) async-start(), calls=%async_computation.13 | async-start | bytes 2097152 | tf_op jit(solution)/shard_map/psum | solution.py:155
  286.6 164.3 %reduce-scatter.15.cloned.1.call-start = ((), (), s32[]{:S(2)}) async-start(), calls=%async_computation.14 | async-start | bytes 1179648 | tf_op jit(solution)/shard_map/reduce_scatter | solution.py:19
  363.9 50.2 %copy-start.4 = (bf16[1024,512]{1,0:T(8,128)(2,1)S(1)}, bf16[1024,512]{1,0:T(8,128)(2,1)}, u32[]{:S(2)}) copy-start(bf16[1024,512]{1,0:T(8,128)(2,1)} %param.23) | copy-start | bytes 3145732
  363.9 51.0 %copy-start.5 = (bf16[1024,512]{1,0:T(8,128)(2,1)S(1)}, bf16[1024,512]{1,0:T(8,128)(2,1)}, u32[]{:S(2)}) copy-start(bf16[1024,512]{1,0:T(8,128)(2,1)} %param.24) | copy-start | bytes 3145732
  386.0 28.0 %copy-start.11 = (bf16[32,4,2,128]{3,2,0,1:T(2,128)(2,1)}, bf16[32,4,2,128]{3,2,0,1:T(2,128)(2,1)S(1)}, u32[]{:S(2)}) copy-start(bf16[32,4,2,128]{3,2,0,1:T(2,128)(2,1)S(1)} %copy.125) | copy-start | bytes 196612
  412.1 58.4 %copy-start.2 = (bf16[4,64,1024]{2,1,0:T(8,128)(2,1)}, bf16[4,64,1024]{2,1,0:T(8,128)(2,1)S(1)}, u32[]{:S(2)}) copy-start(bf16[4,64,1024]{2,1,0:T(8,128)(2,1)S(1)} %all_gather.21) | copy-start | bytes 1572868
  416.3 138.5 %reduce-scatter.17.cloned.1.call-start = ((), (), s32[]{:S(2)}) async-start(), calls=%async_computation.15 | async-start | bytes 1179648 | tf_op jit(solution)/shard_map/reduce_scatter | solution.py:19
  513.3 10.3 %copy-start.8 = (bf16[4,64,512]{2,1,0:T(8,128)(2,1)S(1)}, bf16[4,64,512]{2,1,0:T(8,128)(2,1)}, u32[]{:S(2)}) copy-start(bf16[4,64,512]{2,1,0:T(8,128)(2,1)} %copy-done.7) | copy-start | bytes 786436
  513.3 201.6 %reduce-scatter.19.cloned.1.call-start = ((), (), s32[]{:S(2)}) async-start(), calls=%async_computation.16 | async-start | bytes 8650752
  513.6 10.1 %copy-start.3 = (bf16[4,64,1024]{2,1,0:T(8,128)(2,1)S(1)}, bf16[4,64,1024]{2,1,0:T(8,128)(2,1)}, u32[]{:S(2)}) copy-start(bf16[4,64,1024]{2,1,0:T(8,128)(2,1)} %copy-done.2) | copy-start | bytes 1572868
  534.7 21.2 %copy-start.36 = (f32[128,2]{0,1:T(2,128)S(1)}, f32[128,2]{0,1:T(2,128)}, u32[]{:S(2)}) copy-start(f32[128,2]{0,1:T(2,128)} %get-tuple-element.36) | copy-start | bytes 3076
  534.7 38.5 %copy-start.10 = (bf16[4,64,128]{2,1,0:T(8,128)(2,1)S(1)}, bf16[4,64,128]{2,1,0:T(8,128)(2,1)}, u32[]{:S(2)}) copy-start(bf16[4,64,128]{2,1,0:T(8,128)(2,1)} %copy-done.9) | copy-start | bytes 196612
  534.7 38.5 %copy-start.12 = (f32[4,64,128]{2,1,0:T(8,128)S(1)}, f32[4,64,128]{2,1,0:T(8,128)}, u32[]{:S(2)}) copy-start(f32[4,64,128]{2,1,0:T(8,128)} %get-tuple-element.51) | copy-start | bytes 393220
  574.1 19.9 %all-to-all-start.3 = ((bf16[4,64,128]{2,0,1:T(4,128)(2,1)}), bf16[4,64,128]{2,0,1:T(4,128)(2,1)S(1)}, u32[]{:S(2)}, u32[]{:S(2)}) async-start(bf16[4,64,128]{2,0,1:T(4,128)(2,1)} %concatenate.12.clone), calls=%async_computation.8 | async-start | bytes 131072 | tf_op jit(solution)/shard_map/all_to_all | solution.py:27
  (19 other events, 52.8 us)
Sparse Core Ops, SparseCore 0:
  11.1 43.3 reduce-scatter.8
  108.4 34.4 reduce-scatter.10
  178.3 40.9 reduce-scatter.12
  286.7 77.0 all-reduce.3
  416.4 34.4 reduce-scatter.14
  513.4 41.3 reduce-scatter.16
  559.2 155.6 reduce-scatter.18
where the time goes:
time: 728 us; the launch traced here: 726 us
  waiting for transfers between devices  364 us (50%)
  blocking collectives  230 us (32%)
  matrix products  46 us (6%)
  starting transfers between devices  30.4 us (4%)
  local copies, waits for them, and re-layouts  22.4 us (3%)
  other arithmetic  18.3 us (3%)
  between operations  14.7 us (2%)
    reduce_scatter x5, waiting for transfers between devices, feature_sum(): return lax.psum_scatter(term, 'mp', scatter_dimension=2, tiled=True)  170 us
    all_gather x6, blocking collectives, gather_features(): return lax.all_gather(values, 'mp', axis=2, tiled=True)  161 us
    unnamed x8, waiting for transfers between devices  90.5 us
    psum x1, waiting for transfers between devices, local(): d_final = lax.psum(d_final_part, 'mp')  76.1 us
    psum x2, blocking collectives, local(): lax.psum((jnp.sum(exp_logit, axis=-1), jnp.sum(capped * onehot_f, axis=-1...  31.7 us
    all_to_all x2, starting transfers between devices, rows_to_cols(): return lax.all_to_all(values, 'dp', split_axis=1, concat_axis=0, tiled=True)  20 us
    all_to_all x1, blocking collectives, cols_to_rows(): return lax.all_to_all(values, 'dp', split_axis=0, concat_axis=1, tiled=True)  19.4 us
    all_to_all x2, waiting for transfers between devices, rows_to_cols(): return lax.all_to_all(values, 'dp', split_axis=1, concat_axis=0, tiled=True)  18.7 us
  transfers between devices with their start and end apart: 10, of which 10 were waited for; matrix products, arithmetic and copies ran while one was open for 5% of the time, Pallas kernels for 0%

commit v1 on v0

--- a/solution.py
+++ b/solution.py
@@ -24,7 +24,10 @@
 
 
 def rows_to_cols(values):
-    return lax.all_to_all(values, "dp", split_axis=1, concat_axis=0, tiled=True)
+    return jnp.concatenate(
+        lax.all_to_all(jnp.stack(jnp.split(values, lax.axis_size("dp"), axis=1)), "dp", 0, 0),
+        axis=0,
+    )
 
 
 def rms_of(values):

time: 728 us -> 749 us (1.029)
  local copies, waits for them, and re-layouts: 22.4 us -> 56.7 us
  waiting for transfers between devices: 364 us -> 352 us
    unnamed x86 -> x145, local copies, waits for them, and re-layouts: 12 us -> 47.5 us
    unnamed x8, waiting for transfers between devices: 90.5 us -> 78.4 us
  transfers between devices with their start and end apart: 10 -> 10, of which waited for: 10 -> 10; matrix products, arithmetic and copies ran while one was open for 5% -> 7% of each run, Pallas kernels for 0% -> 0%
where the time goes in v1:
time: 749 us; the launch traced here: 748 us
  waiting for transfers between devices  352 us (47%)
  blocking collectives  230 us (31%)
  local copies, waits for them, and re-layouts  56.7 us (8%)
  matrix products  45.5 us (6%)
  starting transfers between devices  30.1 us (4%)
  other arithmetic  18.6 us (2%)
  between operations  14.7 us (2%)
    reduce_scatter x5, waiting for transfers between devices, feature_sum(): return lax.psum_scatter(term, 'mp', scatter_dimension=2, tiled=True)  171 us
    all_gather x6, blocking collectives, gather_features(): return lax.all_gather(values, 'mp', axis=2, tiled=True)  161 us
    unnamed x8, waiting for transfers between devices  78.4 us
    psum x1, waiting for transfers between devices, local(): d_final = lax.psum(d_final_part, 'mp')  76.1 us
    unnamed x145, local copies, waits for them, and re-layouts  47.5 us
    psum x2, blocking collectives, local(): lax.psum((jnp.sum(exp_logit, axis=-1), jnp.sum(capped * onehot_f, axis=-1...  31.8 us
    all_to_all x2, starting transfers between devices, rows_to_cols(): lax.all_to_all(jnp.stack(jnp.split(values, lax.axis_size('dp'), axis=1)),...  19.6 us
    all_to_all x1, blocking collectives, cols_to_rows(): return lax.all_to_all(values, 'dp', split_axis=0, concat_axis=1, tiled=True)  19.4 us
  transfers between devices with their start and end apart: 10, of which 10 were waited for; matrix products, arithmetic and copies ran while one was open for 7% of the time, Pallas kernels for 0%

profile of v1, /device:TPU:2, one launch (start us, length us, event | category | flops | bytes accessed | tf_op | source)
XLA Modules:
  0.0 747.6 jit_solution(2347491525594593743)
XLA Ops:
  8.0 2.4 convolution_bitcast_fusion
  10.4 44.1 %reduce-scatter.9.cloned.1.call-done = f32[128,2,128]{2,0,1:T(8,128)} async-done(((f32[128,2,1024]{2,0,1:T(8,128)}), f32[128,2,128]{2,0,1:T(8,128)}) %reduce-scatter.9.cloned.1.call-update) | async-done | bytes 131088 | tf_op jit(solution)/shard_map/reduce_scatter | solution.py:19
  56.1 10.0 %all-to-all-start = ((bf16[128,2,128]{2,1,0:T(2,128)(2,1)}), bf16[128,2,128]{2,1,0:T(2,128)(2,1)S(1)}, u32[]{:S(2)}, u32[]{:S(2)}) async-start(bf16[128,2,128]{2,1,0:T(2,128)(2,1)} %copy.112), calls=%async_computation.1 | async-start | bytes 131072 | tf_op jit(solution)/shard_map/all_to_all | solution.py:23
  67.7 8.4 %all-to-all-done = bf16[128,2,128]{2,1,0:T(2,128)(2,1)S(1)} async-done(((bf16[128,2,128]{2,1,0:T(2,128)(2,1)}), bf16[128,2,128]{2,1,0:T(2,128)(2,1)S(1)}, u32[]{:S(2)}, u32[]{:S(2)}) %all-to-all-start) | async-done | bytes 65568 | tf_op jit(solution)/shard_map/all_to_all | solution.py:23
  76.2 26.7 %all_gather.18 = bf16[4,64,1024]{2,1,0:T(8,128)(2,1)S(1)} all-gather(bf16[4,64,128]{2,1,0:T(8,128)(2,1)S(1)} %pad_maximum_fusion.2), channel_id=1, replica_groups=mesh['dp'=32,'mp'=8] {'mp'}, dimensions={2}, use_global_device_ids=true | all-gather | bytes 589824 | tf_op jit(solution)/shard_map/all_gather | solution.py:15
  107.8 34.4 %reduce-scatter.11.cloned.1.call-done = f32[4,64,128]{2,1,0:T(8,128)} async-done(((f32[4,64,1024]{2,1,0:T(8,128)}), f32[4,64,128]{2,1,0:T(8,128)}) %reduce-scatter.11.cloned.1.call-update) | async-done | bytes 131088 | tf_op jit(solution)/shard_map/reduce_scatter | solution.py:19
  143.1 26.9 %all_gather.19 = bf16[4,64,1024]{2,1,0:T(8,128)(2,1)S(1)} all-gather(bf16[4,64,128]{2,1,0:T(8,128)(2,1)S(1)} %fusion.45), channel_id=1, replica_groups=mesh['dp'=32,'mp'=8] {'mp'}, dimensions={2}, use_global_device_ids=true | all-gather | bytes 589824 | tf_op jit(solution)/shard_map/all_gather | solution.py:15
  172.7 2.7 multiply_convert_fusion.3
  177.1 41.0 %reduce-scatter.13.cloned.1.call-done = f32[4,64,128]{2,1,0:T(8,128)} async-done(((f32[4,64,1024]{2,1,0:T(8,128)}), f32[4,64,128]{2,1,0:T(8,128)}) %reduce-scatter.13.cloned.1.call-update) | async-done | bytes 131088 | tf_op jit(solution)/shard_map/reduce_scatter | solution.py:19
  237.7 9.9 %all-to-all-start.1 = ((bf16[32,4,2,128]{3,2,1,0:T(2,128)(2,1)}), bf16[32,4,2,128]{3,2,1,0:T(2,128)(2,1)S(1)}, u32[]{:S(2)}, u32[]{:S(2)}) async-start(bf16[32,4,2,128]{3,2,1,0:T(2,128)(2,1)} %constant_dynamic-update-slice_fusion), calls=%async_computation.4 | async-start | bytes 131072 | tf_op jit(solution)/shard_map/all_to_all | solution.py:28
  248.2 9.3 %all-to-all-done.1 = bf16[32,4,2,128]{3,2,1,0:T(2,128)(2,1)S(1)} async-done(((bf16[32,4,2,128]{3,2,1,0:T(2,128)(2,1)}), bf16[32,4,2,128]{3,2,1,0:T(2,128)(2,1)S(1)}, u32[]{:S(2)}, u32[]{:S(2)}) %all-to-all-start.1) | async-done | bytes 65568 | tf_op jit(solution)/shard_map/all_to_all | solution.py:28
  257.5 26.7 %all_gather.20 = bf16[128,2,1024]{2,0,1:T(8,128)(2,1)S(1)} all-gather(bf16[128,2,128]{2,0,1:T(8,128)(2,1)S(1)} %copy.119), channel_id=1, replica_groups=mesh['dp'=32,'mp'=8] {'mp'}, dimensions={2}, use_global_device_ids=true | all-gather | bytes 589824 | tf_op jit(solution)/shard_map/all_gather | solution.py:15
  286.6 14.4 %psum.35 = f32[128,2]{0,1:T(2,128)S(1)} all-reduce(f32[128,2]{0,1:T(2,128)} %get-tuple-element.35), channel_id=1, replica_groups=mesh['dp'=32,'mp'=8] {'mp'}, use_global_device_ids=true, to_apply=%region_8.9 | all-reduce | flops 256 | bytes 2048 | tf_op jit(solution)/shard_map/psum | solution.py:139
  304.4 76.1 %all-reduce.4.cloned.1.call-done = f32[128,2,1024]{2,0,1:T(8,128)} async-done(((f32[128,2,1024]{2,0,1:T(8,128)}), f32[128,2,1024]{2,0,1:T(8,128)}) %all-reduce.4.cloned.1.call-update) | async-done | bytes 1048592 | tf_op jit(solution)/shard_map/psum | solution.py:158
  383.3 19.4 %all_to_all.46 = bf16[128,2,128]{2,1,0:T(2,128)(2,1)S(1)} all-to-all(bf16[128,2,128]{2,1,0:T(2,128)(2,1)S(1)} %copy.121), channel_id=1, replica_groups=mesh['dp'=32,'mp'=8] {'dp'}, dimensions={0} | all-to-all | bytes 131072 | tf_op jit(solution)/shard_map/all_to_all | solution.py:23
  402.7 26.0 %all_gather.21 = bf16[4,64,1024]{2,1,0:T(8,128)(2,1)S(1)} all-gather(bf16[4,64,128]{2,1,0:T(8,128)(2,1)S(1)} %bitcast.389), channel_id=1, replica_groups=mesh['dp'=32,'mp'=8] {'mp'}, dimensions={2}, use_global_device_ids=true | all-gather | bytes 589824 | tf_op jit(solution)/shard_map/all_gather | solution.py:15
  434.2 33.3 %reduce-scatter.15.cloned.1.call-done = f32[4,64,128]{2,1,0:T(8,128)} async-done(((f32[4,64,1024]{2,1,0:T(8,128)}), f32[4,64,128]{2,1,0:T(8,128)}) %reduce-scatter.15.cloned.1.call-update) | async-done | bytes 131088 | tf_op jit(solution)/shard_map/reduce_scatter | solution.py:19
  469.1 18.0 %psum.38 = f32[4,64]{1,0:T(4,128)} all-reduce(f32[4,64]{1,0:T(4,128)} %fusion.51), channel_id=1, replica_groups=mesh['dp'=32,'mp'=8] {'mp'}, use_global_device_ids=true, to_apply=%region_16.17 | all-reduce | flops 256 | bytes 2048 | tf_op jit(solution)/shard_map/psum | solution.py:53
  488.9 26.8 %all_gather.22 = bf16[4,64,1024]{2,1,0:T(8,128)(2,1)S(1)} all-gather(bf16[4,64,128]{2,1,0:T(8,128)(2,1)S(1)} %fusion.63), channel_id=1, replica_groups=mesh['dp'=32,'mp'=8] {'mp'}, dimensions={2}, use_global_device_ids=true | all-gather | bytes 589824 | tf_op jit(solution)/shard_map/all_gather | solution.py:15
  519.5 2.2 convolution_convert_fusion.2
  525.7 2.6 convolution_bitcast_fusion.1
  528.6 2.6 bitcast_dynamic-update-slice_fusion.3
  533.2 2.8 bitcast_dynamic-update-slice_fusion.2
  536.0 2.6 bitcast_dynamic-update-slice_fusion.1
  540.4 9.2 %copy.152 = f32[1024,2048]{1,0:T(8,128)} copy(f32[1024,2048]{0,1:T(8,128)} %bitcast_dynamic-update-slice_fusion) | data formatting | bytes 16777216
  552.0 17.9 %reduce-scatter.17.cloned.1.call-done = f32[4,64,128]{2,1,0:T(8,128)} async-done(((f32[4,64,1024]{2,1,0:T(8,128)}), f32[4,64,128]{2,1,0:T(8,128)}) %reduce-scatter.17.cloned.1.call-update) | async-done | bytes 131088 | tf_op jit(solution)/shard_map/reduce_scatter | solution.py:19
  570.9 17.4 %all-reduce.1 = (f32[128,2]{0,1:T(2,128)S(1)}, f32[4,64]{1,0:T(4,128)S(1)}) all-reduce(f32[128,2]{0,1:T(2,128)S(1)} %copy-done.35, f32[4,64]{1,0:T(4,128)S(1)} %fusion.46), channel_id=1, replica_groups=mesh['dp'=32,'mp'=8] {'mp'}, use_global_device_ids=true, to_apply=%region_10.11 | all-reduce | flops 512 | bytes 4096 | tf_op jit(solution)/shard_map/psum | solution.py:139
  608.1 9.7 %all-to-all-start.3 = ((bf16[32,4,2,128]{3,2,1,0:T(2,128)(2,1)}), bf16[32,4,2,128]{3,2,1,0:T(2,128)(2,1)S(1)}, u32[]{:S(2)}, u32[]{:S(2)}) async-start(bf16[32,4,2,128]{3,2,1,0:T(2,128)(2,1)} %constant_dynamic-update-slice_fusion.32), calls=%async_computation.8 | async-start | bytes 131072 | tf_op jit(solution)/shard_map/all_to_all | solution.py:28
  618.4 9.4 %all-to-all-done.3 = bf16[32,4,2,128]{3,2,1,0:T(2,128)(2,1)S(1)} async-done(((bf16[32,4,2,128]{3,2,1,0:T(2,128)(2,1)}), bf16[32,4,2,128]{3,2,1,0:T(2,128)(2,1)S(1)}, u32[]{:S(2)}, u32[]{:S(2)}) %all-to-all-start.3) | async-done | bytes 65568 | tf_op jit(solution)/shard_map/all_to_all | solution.py:28
  627.8 27.5 %all_gather.23 = bf16[128,2,1024]{2,0,1:T(8,128)(2,1)S(1)} all-gather(bf16[128,2,128]{2,0,1:T(8,128)(2,1)S(1)} %copy.134), channel_id=1, replica_groups=mesh['dp'=32,'mp'=8] {'mp'}, dimensions={2}, use_global_device_ids=true | all-gather | bytes 589824 | tf_op jit(solution)/shard_map/all_gather | solution.py:15
  655.3 2.5 convolution_add_fusion
  657.8 78.3 %reduce-scatter.19.cloned.1.call-done = f32[32,2048]{1,0:T(8,128)} async-done(((f32[1024,2048]{1,0:T(8,128)}), f32[32,2048]{1,0:T(8,128)}) %reduce-scatter.19.cloned.1.call-update) | async-done | bytes 262160
  (226 shorter events, 91.6 us)
Async XLA Ops:
  7.2 168.2 %copy-start = (bf16[1024,512]{1,0:T(8,128)(2,1)S(1)}, bf16[1024,512]{1,0:T(8,128)(2,1)}, u32[]{:S(2)}) copy-start(bf16[1024,512]{1,0:T(8,128)(2,1)} %param.25) | copy-start | bytes 3145732
  7.2 99.2 %copy-start.6 = (bf16[1024,128]{1,0:T(8,128)(2,1)S(1)}, bf16[1024,128]{1,0:T(8,128)(2,1)}, u32[]{:S(2)}) copy-start(bf16[1024,128]{1,0:T(8,128)(2,1)} %param.22) | copy-start | bytes 786436
  7.2 100.6 %copy-start.34 = (bf16[1024]{0:T(1024)(128)(2,1)S(1)}, bf16[1024]{0:T(1024)(128)(2,1)}, u32[]{:S(2)}) copy-start(bf16[1024]{0:T(1024)(128)(2,1)} %param.19) | copy-start | bytes 6148
  7.2 47.3 %reduce-scatter.9.cloned.1.call-start = ((), (), s32[]{:S(2)}) async-start(), calls=%async_computation.10 | async-start | bytes 1179648 | tf_op jit(solution)/shard_map/reduce_scatter | solution.py:19
  56.1 20.0 %all-to-all-start = ((bf16[128,2,128]{2,1,0:T(2,128)(2,1)}), bf16[128,2,128]{2,1,0:T(2,128)(2,1)S(1)}, u32[]{:S(2)}, u32[]{:S(2)}) async-start(bf16[128,2,128]{2,1,0:T(2,128)(2,1)} %copy.112), calls=%async_computation.1 | async-start | bytes 131072 | tf_op jit(solution)/shard_map/all_to_all | solution.py:23
  66.1 76.0 %reduce-scatter.11.cloned.1.call-start = ((), (), s32[]{:S(2)}) async-start(), calls=%async_computation.11 | async-start | bytes 1179648 | tf_op jit(solution)/shard_map/reduce_scatter | solution.py:19
  66.9 38.6 %copy-start.29 = (f32[1024]{0:T(1024)}, f32[1024]{0:T(1024)S(1)}, u32[]{:S(2)}) copy-start(f32[1024]{0:T(1024)S(1)} %convert_element_type.117) | copy-start | bytes 12292
  67.7 74.5 %copy-start.27 = (pred[64,64]{0,1:T(8,128)(4,1)}, pred[64,64]{0,1:T(8,128)(4,1)S(1)}, u32[]{:S(2)}) copy-start(pred[64,64]{0,1:T(8,128)(4,1)S(1)} %iota_compare_fusion.3) | copy-start | bytes 12292
  103.7 69.0 %copy-start.23 = (f32[4,64]{1,0:T(4,128)}, f32[4,64]{1,0:T(4,128)S(1)}, u32[]{:S(2)}) copy-start(f32[4,64]{1,0:T(4,128)S(1)} %get-tuple-element.50) | copy-start | bytes 3076
  105.6 36.6 %copy-start.21 = (bf16[4,64,1,128]{1,3,0,2:T(8,128)(2,1)}, bf16[4,64,1,128]{1,3,0,2:T(8,128)(2,1)S(1)}, u32[]{:S(2)}) copy-start(bf16[4,64,1,128]{1,3,0,2:T(8,128)(2,1)S(1)} %copy.160) | copy-start | bytes 196612
  105.7 36.4 %copy-start.12 = (bf16[4,64,2,64]{3,2,1,0:T(2,128)(2,1)}, bf16[4,64,2,64]{3,2,1,0:T(2,128)(2,1)S(1)}, u32[]{:S(2)}) copy-start(bf16[4,64,2,64]{3,2,1,0:T(2,128)(2,1)S(1)} %reshape_squeeze.9) | copy-start | bytes 196612
  106.0 64.8 %copy-start.38 = (f32[4,2,64]{2,1,0:T(2,128)}, f32[4,2,64]{2,1,0:T(2,128)S(1)}, u32[]{:S(2)}) copy-start(f32[4,2,64]{2,1,0:T(2,128)S(1)} %get-tuple-element.55) | copy-start | bytes 6148
  106.4 35.8 %copy-start.13 = (bf16[4,2,64,64]{3,2,1,0:T(8,128)(2,1)}, bf16[4,2,64,64]{3,2,1,0:T(8,128)(2,1)S(1)}, u32[]{:S(2)}) copy-start(bf16[4,2,64,64]{3,2,1,0:T(8,128)(2,1)S(1)} %convolution_convert_fusion.4) | copy-start | bytes 196612
  107.7 110.4 %reduce-scatter.13.cloned.1.call-start = ((), (), s32[]{:S(2)}) async-start(), calls=%async_computation.12 | async-start | bytes 1179648 | tf_op jit(solution)/shard_map/reduce_scatter | solution.py:19
  107.8 69.0 %copy-start.30 = (f32[1024]{0:T(1024)}, f32[1024]{0:T(1024)S(1)}, u32[]{:S(2)}) copy-start(f32[1024]{0:T(1024)S(1)} %convert_element_type.126) | copy-start | bytes 12292
  170.8 114.1 %copy-start.1 = (bf16[2,128,1024]{2,1,0:T(8,128)(2,1)S(1)}, bf16[2,128,1024]{2,1,0:T(8,128)(2,1)}, u32[]{:S(2)}) copy-start(bf16[2,128,1024]{2,1,0:T(8,128)(2,1)} %param.16) | copy-start | bytes 1572868
  175.4 82.1 %copy-start.7 = (bf16[4,64,512]{2,1,0:T(8,128)(2,1)}, bf16[4,64,512]{2,1,0:T(8,128)(2,1)S(1)}, u32[]{:S(2)}) copy-start(bf16[4,64,512]{2,1,0:T(8,128)(2,1)S(1)} %get-tuple-element.57) | copy-start | bytes 786436
  237.7 19.8 %all-to-all-start.1 = ((bf16[32,4,2,128]{3,2,1,0:T(2,128)(2,1)}), bf16[32,4,2,128]{3,2,1,0:T(2,128)(2,1)S(1)}, u32[]{:S(2)}, u32[]{:S(2)}) async-start(bf16[32,4,2,128]{3,2,1,0:T(2,128)(2,1)} %constant_dynamic-update-slice_fusion), calls=%async_computation.4 | async-start | bytes 131072 | tf_op jit(solution)/shard_map/all_to_all | solution.py:28
  247.6 132.9 %all-reduce.4.cloned.1.call-start = ((), (), s32[]{:S(2)}) async-start(), calls=%async_computation.13 | async-start | bytes 2097152 | tf_op jit(solution)/shard_map/psum | solution.py:158
  303.3 164.2 %reduce-scatter.15.cloned.1.call-start = ((), (), s32[]{:S(2)}) async-start(), calls=%async_computation.14 | async-start | bytes 1179648 | tf_op jit(solution)/shard_map/reduce_scatter | solution.py:19
  380.5 50.2 %copy-start.4 = (bf16[1024,512]{1,0:T(8,128)(2,1)S(1)}, bf16[1024,512]{1,0:T(8,128)(2,1)}, u32[]{:S(2)}) copy-start(bf16[1024,512]{1,0:T(8,128)(2,1)} %param.23) | copy-start | bytes 3145732
  380.5 51.0 %copy-start.5 = (bf16[1024,512]{1,0:T(8,128)(2,1)S(1)}, bf16[1024,512]{1,0:T(8,128)(2,1)}, u32[]{:S(2)}) copy-start(bf16[1024,512]{1,0:T(8,128)(2,1)} %param.24) | copy-start | bytes 3145732
  402.7 28.0 %copy-start.9 = (bf16[32,4,2,128]{3,2,0,1:T(2,128)(2,1)}, bf16[32,4,2,128]{3,2,0,1:T(2,128)(2,1)S(1)}, u32[]{:S(2)}) copy-start(bf16[32,4,2,128]{3,2,0,1:T(2,128)(2,1)S(1)} %copy.122) | copy-start | bytes 196612
  428.7 58.4 %copy-start.2 = (bf16[4,64,1024]{2,1,0:T(8,128)(2,1)}, bf16[4,64,1024]{2,1,0:T(8,128)(2,1)S(1)}, u32[]{:S(2)}) copy-start(bf16[4,64,1024]{2,1,0:T(8,128)(2,1)S(1)} %all_gather.21) | copy-start | bytes 1572868
  432.9 136.9 %reduce-scatter.17.cloned.1.call-start = ((), (), s32[]{:S(2)}) async-start(), calls=%async_computation.15 | async-start | bytes 1179648 | tf_op jit(solution)/shard_map/reduce_scatter | solution.py:19
  528.3 10.3 %copy-start.8 = (bf16[4,64,512]{2,1,0:T(8,128)(2,1)S(1)}, bf16[4,64,512]{2,1,0:T(8,128)(2,1)}, u32[]{:S(2)}) copy-start(bf16[4,64,512]{2,1,0:T(8,128)(2,1)} %copy-done.7) | copy-start | bytes 786436
  528.3 207.8 %reduce-scatter.19.cloned.1.call-start = ((), (), s32[]{:S(2)}) async-start(), calls=%async_computation.16 | async-start | bytes 8650752
  549.6 21.3 %copy-start.35 = (f32[128,2]{0,1:T(2,128)S(1)}, f32[128,2]{0,1:T(2,128)}, u32[]{:S(2)}) copy-start(f32[128,2]{0,1:T(2,128)} %get-tuple-element.36) | copy-start | bytes 3076
  549.6 38.7 %copy-start.11 = (bf16[4,64,128]{2,1,0:T(8,128)(2,1)S(1)}, bf16[4,64,128]{2,1,0:T(8,128)(2,1)}, u32[]{:S(2)}) copy-start(bf16[4,64,128]{2,1,0:T(8,128)(2,1)} %copy-done.10) | copy-start | bytes 196612
  549.6 38.7 %copy-start.22 = (f32[4,64]{1,0:T(4,128)S(1)}, f32[4,64]{1,0:T(4,128)}, u32[]{:S(2)}) copy-start(f32[4,64]{1,0:T(4,128)} %get-tuple-element.49) | copy-start | bytes 3076
  549.7 38.7 %copy-start.24 = (f32[4,64]{1,0:T(4,128)S(1)}, f32[4,64]{1,0:T(4,128)}, u32[]{:S(2)}) copy-start(f32[4,64]{1,0:T(4,128)} %copy-done.23) | copy-start | bytes 3076
  608.1 19.7 %all-to-all-start.3 = ((bf16[32,4,2,128]{3,2,1,0:T(2,128)(2,1)}), bf16[32,4,2,128]{3,2,1,0:T(2,128)(2,1)S(1)}, u32[]{:S(2)}, u32[]{:S(2)}) async-start(bf16[32,4,2,128]{3,2,1,0:T(2,128)(2,1)} %constant_dynamic-update-slice_fusion.32), calls=%async_computation.8 | async-start | bytes 131072 | tf_op jit(solution)/shard_map/all_to_all | solution.py:28
  (18 other events, 59.7 us)
Sparse Core Ops, SparseCore 0:
  11.1 43.3 reduce-scatter.8
  107.8 34.2 reduce-scatter.10
  177.0 41.0 reduce-scatter.12
  303.4 77.0 all-reduce.3
  433.0 34.4 reduce-scatter.14
  528.4 41.4 reduce-scatter.16
  574.3 161.8 reduce-scatter.18
